TPU v7x, 256 devices: a whole 4x4x8 slice. The times are simulated.
256 devices in a mesh: samp: 8 (over x, core), var: 32 (over z, y).
Axes of the slice: x: 4, y: 4, z: 8, core: 2. Of those that a mesh axis runs over, the one named last changes fastest.
Arguments:
- phenotype: bfloat16 [65536, 256], P(('samp', 'var')), may hold values from -1500 to 1500
- inverse_blocks: float32 [256, 256, 256], P(('samp', 'var')), may hold values from -1 to 2, as said below
- bin_sizes: int32 [8, 32], P('samp', 'var'), may hold values from 128 to 256, as said below
- slot_of: int32 [49152], P('samp'), may hold values from 0 to 8191, as said below
- dosages: bfloat16 [49152, 32768], P('samp', 'var'), may hold values from 0 to 2
Outputs:
- z_scores: float32 [32768, 256], P('var', 'samp')
Inputs may be any that keep to these rules, and one draw needn't show every extreme that they name: `bin_sizes`: within each row (one sample shard) the sizes sum to 192 times the row's length, and at least one bin is full. `slot_of`: within each sample shard the samples occupy exactly the live slots: slot v * 256 + r with r < bin_sizes of bin v, each once. `inverse_blocks`: each block is symmetric positive definite.
All inputs are finite; a program needn't handle non-finite values.
Results may differ from a plain program's by a relative error of at most 0.0041.
Values may be sent and summed in bfloat16 or wider, within the bound.
A program may use at most 128 MiB of HBM per device.

v0:
```python
import jax
import jax.numpy as jnp
from jax import lax
from jax.sharding import Mesh
from jax.sharding import PartitionSpec as P

SAMP_VAR = ("samp_0", "samp_1", "var_0", "var_1")
VAR = ("var_0", "var_1")
SAMP = ("samp_0", "samp_1")
epsilon = 1e-06


def one_axis_at_a_time(value, axes):
    for axis in axes:
        value = lax.psum(value, axis)
    return value


def gather_axes(value, axes, dim):
    if not axes:
        return value
    nearer = lax.all_gather(value, axes[-1], axis=dim, tiled=True)
    return gather_axes(nearer, axes[:-1], dim)


def in_blocks(value, dim, peers):
    before, after = (value.shape[:dim], value.shape[dim + 1 :])
    return jnp.moveaxis(value.reshape(*before, peers, -1, *after), dim, 0)


def sent_and_summed(value, axis, dim):
    peers = lax.axis_size(axis)
    pieces = lax.all_to_all(in_blocks(value, dim, peers), axis, 0, 0, tiled=True)
    return jnp.sum(pieces.astype(jnp.float32), axis=0)


def copy_for_each(value, axis):
    peers = lax.axis_size(axis)
    return lax.all_to_all(
        jnp.broadcast_to(value[None], (peers, *value.shape)), axis, 0, 0, tiled=True
    )


def taken_together(value, axis):
    return copy_for_each(value, axis).sum(axis=0)


def local(phenotype, inverse_blocks, bin_sizes, slot_of, dosages):
    bin_width = inverse_blocks.shape[1]
    position = jnp.arange(bin_width, dtype=jnp.int32)
    live_mask = (position < bin_sizes.reshape(())).astype(jnp.float32)[:, None]
    masked_pheno = phenotype.astype(jnp.float32) * live_mask
    whitened = (
        jnp.dot(
            inverse_blocks[0],
            masked_pheno,
            precision=lax.Precision.HIGHEST,
            preferred_element_type=jnp.float32,
        )
        * live_mask
    )
    trait_scale = one_axis_at_a_time(jnp.sum(masked_pheno * whitened, axis=0), SAMP_VAR)
    white_rows = whitened.astype(jnp.bfloat16)
    slot_weight = jnp.diagonal(inverse_blocks[0]).astype(jnp.bfloat16)
    gathered, weights_all = (gather_axes(white_rows, VAR, 0), gather_axes(slot_weight, VAR, 0))
    picked = jnp.take(gathered, slot_of, axis=0)
    score_part = lax.dot_general(
        dosages, picked, (((0,), (0,)), ((), ())), preferred_element_type=jnp.float32
    )
    sample_weight = jnp.take(weights_all, slot_of).astype(jnp.float32)
    variance = jnp.dot(
        sample_weight, dosages.astype(jnp.float32) ** 2, precision=lax.Precision.HIGHEST
    )
    trait_count = phenotype.shape[1] // lax.axis_size(SAMP)
    trait_start = lax.axis_index(SAMP) * trait_count
    score_share = sent_and_summed(score_part.astype(jnp.bfloat16), SAMP, 1)
    variance_all = taken_together(variance, SAMP)
    scale_share = lax.dynamic_slice_in_dim(trait_scale, trait_start, trait_count, 0)
    sample_count = slot_of.shape[0] * lax.axis_size(SAMP)
    return score_share / jnp.sqrt(
        variance_all[:, None] * scale_share[None, :] / sample_count + epsilon
    )


def solution(mesh):
    split = Mesh(mesh.devices.reshape(4, 2, 8, 4), ("samp_0", "samp_1", "var_0", "var_1"))
    in_specs = (P(SAMP_VAR, None), P(SAMP_VAR, None, None), P(SAMP, VAR), P(SAMP), P(SAMP, VAR))
    out_specs = P(VAR, SAMP)
    return jax.shard_map(local, mesh=split, in_specs=in_specs, out_specs=out_specs, check_vma=False)
```

profile of v0, /device:TPU:8, one launch (start us, length us, event | category | flops | bytes accessed | tf_op | source)
XLA Modules:
  0.0 200.2 jit_solution(13679015611097144882)
XLA Ops:
  6.5 0.0 copy-start
  6.5 0.0 all-gather.3.cloned.1.call-start
  7.2 0.3 copy-done
  7.5 1.5 multiply_reduce_fusion
  9.0 14.4 %all_gather.12 = bf16[1024,256]{1,0:T(8,128)(2,1)} all-gather(bf16[256,256]{1,0:T(8,128)(2,1)S(1)} %get-tuple-element.8), channel_id=1, replica_groups=mesh['samp_0'=4,'samp_1'=2,'var_0'=8,'var_1'=4] {'var_1'}, dimensions={0}, use_global_device_ids=true | all-gather | bytes 655360 | tf_op jit(solution)/shard_map/all_gather | solution.py:22
  23.4 0.0 all-gather.3.cloned.1.call-update
  23.4 2.3 %gather_fusion.1 = bf16[256]{0:T(256)(128)(2,1)S(1)} fusion(f32[256,256]{1,0:T(8,128)S(1)} %bitcast.20, s32[256]{0:T(256)S(1)} %bitcast.21), kind=kCustom, calls=%fused_computation.1 | custom fusion | bytes 3072 | tf_op jit(solution)/shard_map/jit(diagonal)/cond/branch_0_fun/gather | solution.py:64
  25.8 8.5 %all-gather = bf16[4,1,256]{2,1,0:T(2,128)(2,1)S(1)} all-gather(bf16[1,1,256]{2,1,0:T(2,128)(2,1)S(1)} %reshape.50), channel_id=1, replica_groups=mesh['samp_0'=4,'samp_1'=2,'var_0'=8,'var_1'=4] {'var_1'}, dimensions={0}, use_global_device_ids=true | all-gather | bytes 2560 | tf_op jit(solution)/shard_map/all_gather | solution.py:22
  34.4 24.0 %all_gather.15 = bf16[8192]{0:T(1024)(128)(2,1)S(1)} all-gather(bf16[1024]{0:T(1024)(128)(2,1)S(1)} %bitcast.24), channel_id=1, replica_groups=mesh['samp_0'=4,'samp_1'=2,'var_0'=8,'var_1'=4] {'var_0'}, dimensions={0}, use_global_device_ids=true | all-gather | bytes 18432 | tf_op jit(solution)/shard_map/all_gather | solution.py:22
  58.4 0.7 fusion.12
  59.1 0.0 copy-start.1
  59.1 38.2 %gather_fusion.2 = bf16[6144]{0:T(1024)(128)(2,1)S(1)} fusion(bf16[8192]{0:T(1024)(128)(2,1)S(1)} %all_gather.15, s32[6144]{0:T(1024)S(1)} %fusion.12), kind=kCustom, calls=%fused_computation.2 | custom fusion | bytes 49152 | tf_op jit(solution)/shard_map/jit(_take)/gather | solution.py:70
  97.3 0.0 copy-done.1
  97.4 12.3 %fusion = f32[1,1024]{1,0:T(1,128)S(1)} fusion(bf16[6144,1]{0,1:T(2,128)(2,1)S(1)} %reshape.52, bf16[6144,1024]{1,0:T(8,128)(2,1)} %param.9), kind=kOutput, calls=%fused_computation.3 | convolution fusion | flops 88080384 | bytes 12599296 | tf_op jit(solution)/shard_map/dot_general | solution.py:71
  109.7 0.6 broadcast_in_dim.35
  110.3 4.3 %all-to-all-start.1 = ((f32[8,1,1024]{2,1,0:T(1,128)}), f32[8,1,1024]{2,1,0:T(1,128)S(1)}, u32[]{:S(2)}, u32[]{:S(2)}) async-start(f32[8,1,1024]{2,1,0:T(1,128)} %broadcast_in_dim.35), calls=%async_computation.1 | async-start | bytes 65536 | tf_op jit(solution)/shard_map/all_to_all | solution.py:39
  114.6 0.0 all-gather.3.cloned.1.call-done
  114.6 22.1 %gather_fusion = bf16[6144,256]{1,0:T(8,128)(2,1)S(1)} fusion(bf16[8192,256]{1,0:T(8,128)(2,1)} %all-gather.3.cloned.1.call-done, s32[6144]{0:T(1024)S(1)} %fusion.12), kind=kCustom, calls=%fused_computation | custom fusion | bytes 6316032 | tf_op jit(solution)/shard_map/jit(_take)/gather | solution.py:66
  136.7 9.7 %fusion.7 = bf16[256,1024]{1,0:T(8,128)(2,1)} fusion(bf16[6144,1024]{1,0:T(8,128)(2,1)} %param.9, bf16[6144,256]{1,0:T(8,128)(2,1)S(1)} %gather_fusion, pred[6144]{0:T(1024)(128)(4,1)S(1)} %get-tuple-element.6), kind=kOutput, calls=%fused_computation.10 | convolution fusion | flops 3223060480 | bytes 16259072 | tf_op jit(solution)/shard_map/dot_general | solution.py:67
  146.4 0.0 all-to-all-done.1
  146.4 4.8 %all-to-all-start = ((bf16[8,1024,32]{1,2,0:T(8,128)(2,1)}), bf16[8,1024,32]{1,2,0:T(8,128)(2,1)S(1)}, u32[]{:S(2)}, u32[]{:S(2)}) async-start(bf16[8,1024,32]{1,2,0:T(8,128)(2,1)} %bitcast.22), calls=%async_computation | async-start | bytes 1048576 | tf_op jit(solution)/shard_map/all_to_all | solution.py:33
  151.2 12.6 %psum.28 = f32[256]{0:T(256)S(1)} all-reduce(f32[256]{0:T(256)S(1)} %get-tuple-element.7), channel_id=1, replica_groups=mesh['samp_0'=4,'samp_1'=2,'var_0'=8,'var_1'=4] {'samp_0'}, use_global_device_ids=true, to_apply=%region_3.0 | all-reduce | flops 256 | bytes 2048 | tf_op jit(solution)/shard_map/psum | solution.py:15
  163.8 2.4 %psum.29 = f32[256]{0:T(256)S(1)} all-reduce(f32[256]{0:T(256)S(1)} %psum.28), channel_id=1, replica_groups=mesh['samp_0'=4,'samp_1'=2,'var_0'=8,'var_1'=4] {'samp_1'}, use_global_device_ids=true, to_apply=%region_4.0 | all-reduce | flops 256 | bytes 2048 | tf_op jit(solution)/shard_map/psum | solution.py:15
  166.2 15.4 %psum.30 = f32[256]{0:T(256)S(1)} all-reduce(f32[256]{0:T(256)S(1)} %psum.29), channel_id=1, replica_groups=mesh['samp_0'=4,'samp_1'=2,'var_0'=8,'var_1'=4] {'var_0'}, use_global_device_ids=true, to_apply=%region_5.6 | all-reduce | flops 256 | bytes 2048 | tf_op jit(solution)/shard_map/psum | solution.py:15
  181.6 10.8 %psum.31 = f32[256]{0:T(256)S(1)} all-reduce(f32[256]{0:T(256)S(1)} %psum.30), channel_id=1, replica_groups=mesh['samp_0'=4,'samp_1'=2,'var_0'=8,'var_1'=4] {'var_1'}, use_global_device_ids=true, to_apply=%region_6.7 | all-reduce | flops 256 | bytes 2048 | tf_op jit(solution)/shard_map/psum | solution.py:15
  192.4 0.1 dynamic_slice.3
  192.5 0.0 all-to-all-done
  192.5 0.1 convert_reduce_fusion
  192.6 0.8 rsqrt_multiply_fusion
  (8 shorter events, 0.1 us)
Async XLA Ops:
  6.5 1.0 copy-start
  6.5 108.1 %all-gather.3.cloned.1.call-start = ((), (), s32[]{:S(2)}) async-start(), calls=%async_computation.2 | async-start | bytes 4718592 | tf_op jit(solution)/shard_map/all_gather | solution.py:22
  59.1 38.2 %copy-start.1 = (s32[6144]{0:T(1024)S(1)}, s32[6144]{0:T(1024)}, u32[]{:S(2)}) copy-start(s32[6144]{0:T(1024)} %param.8) | copy-start | bytes 73732
  110.3 36.1 %all-to-all-start.1 = ((f32[8,1,1024]{2,1,0:T(1,128)}), f32[8,1,1024]{2,1,0:T(1,128)S(1)}, u32[]{:S(2)}, u32[]{:S(2)}) async-start(f32[8,1,1024]{2,1,0:T(1,128)} %broadcast_in_dim.35), calls=%async_computation.1 | async-start | bytes 65536 | tf_op jit(solution)/shard_map/all_to_all | solution.py:39
  146.4 46.1 %all-to-all-start = ((bf16[8,1024,32]{1,2,0:T(8,128)(2,1)}), bf16[8,1024,32]{1,2,0:T(8,128)(2,1)S(1)}, u32[]{:S(2)}, u32[]{:S(2)}) async-start(bf16[8,1024,32]{1,2,0:T(8,128)(2,1)} %bitcast.22), calls=%async_computation | async-start | bytes 1048576 | tf_op jit(solution)/shard_map/all_to_all | solution.py:33
Sparse Core Ops, SparseCore 0:
  23.5 57.5 all-gather.2
where the time goes:
time: 201 us; the launch traced here: 200 us
  blocking collectives  88.2 us (44%)
  local copies, waits for them, and re-layouts  63.6 us (32%)
  matrix products  23.4 us (12%)
  between operations  14.2 us (7%)
  starting transfers between devices  9.07 us (5%)
    all_gather x3, blocking collectives, gather_axes(): nearer = lax.all_gather(value, axes[-1], axis=dim, tiled=True)  47 us
    psum x4, blocking collectives, one_axis_at_a_time(): value = lax.psum(value, axis)  41.3 us
    gather x1, local copies, waits for them, and re-layouts, local(): sample_weight = jnp.take(weights_all, slot_of).astype(jnp.float32)  38.2 us
    gather x1, local copies, waits for them, and re-layouts, local(): picked = jnp.take(gathered, slot_of, axis=0)  22.1 us
    dot_general x1, matrix products, local(): jnp.dot(sample_weight, dosages.astype(jnp.float32) ** 2, precision=lax.Pr...  12.3 us
    dot_general x1, matrix products, local(): lax.dot_general(dosages, picked, (((0,), (0,)), ((), ())), preferred_elem...  9.66 us
    all_to_all x1, starting transfers between devices, sent_and_summed(): lax.all_to_all(in_blocks(value, dim, peers), axis, 0, 0, tiled=True)  4.78 us
    all_to_all x1, starting transfers between devices, copy_for_each(): lax.all_to_all(jnp.broadcast_to(value[None], (peers, *value.shape)), axis...  4.29 us
  transfers between devices with their start and end apart: 3, of which 0 were waited for; matrix products, arithmetic and copies ran while one was open for 43% of the time, Pallas kernels for 0%

commit v1 on v0

--- a/solution.py
+++ b/solution.py
@@ -12,7 +12,7 @@
 
 def one_axis_at_a_time(value, axes):
     for axis in axes:
-        value = lax.psum(value, axis)
+        value = jnp.sum(lax.all_gather(value, axis), axis=0)
     return value
 
 

time: 201 us -> 198 us (0.985)
  blocking collectives: 88.2 us -> 85.8 us
    psum x4 -> x0, blocking collectives: 41.3 us -> none  [one_axis_at_a_time(): value = lax.psum(value, axis)]
    all_gather x0 -> x4, blocking collectives: none -> 38.9 us  [one_axis_at_a_time(): value = jnp.sum(lax.all_gather(value, axis), axis=0)]
  transfers between devices with their start and end apart: 3 -> 3, of which waited for: 0 -> 0; matrix products, arithmetic and copies ran while one was open for 43% -> 44% of each run, Pallas kernels for 0% -> 0%
where the time goes in v1:
time: 198 us
  blocking collectives  85.8 us (43%)
  local copies, waits for them, and re-layouts  63.6 us (32%)
  matrix products  23.4 us (12%)
  between operations  14.2 us (7%)
  starting transfers between devices  9.07 us (5%)
    all_gather x3, blocking collectives, gather_axes(): nearer = lax.all_gather(value, axes[-1], axis=dim, tiled=True)  47 us
    all_gather x4, blocking collectives, one_axis_at_a_time(): value = jnp.sum(lax.all_gather(value, axis), axis=0)  38.9 us
    gather x1, local copies, waits for them, and re-layouts, local(): sample_weight = jnp.take(weights_all, slot_of).astype(jnp.float32)  38.2 us
    gather x1, local copies, waits for them, and re-layouts, local(): picked = jnp.take(gathered, slot_of, axis=0)  22.1 us
    dot_general x1, matrix products, local(): jnp.dot(sample_weight, dosages.astype(jnp.float32) ** 2, precision=lax.Pr...  12.3 us
    dot_general x1, matrix products, local(): lax.dot_general(dosages, picked, (((0,), (0,)), ((), ())), preferred_elem...  9.66 us
    all_to_all x1, starting transfers between devices, sent_and_summed(): lax.all_to_all(in_blocks(value, dim, peers), axis, 0, 0, tiled=True)  4.78 us
    all_to_all x1, starting transfers between devices, copy_for_each(): lax.all_to_all(jnp.broadcast_to(value[None], (peers, *value.shape)), axis...  4.29 us
  transfers between devices with their start and end apart: 3, of which 0 were waited for; matrix products, arithmetic and copies ran while one was open for 44% of the time, Pallas kernels for 0%

profile of v1, /device:TPU:8, one launch (start us, length us, event | category | flops | bytes accessed | tf_op | source)
XLA Modules:
  0.0 197.9 jit_solution(5238973402900472335)
XLA Ops:
  6.5 0.0 copy-start
  6.5 0.0 all-gather.11.cloned.1.call-start
  7.2 0.3 copy-done
  7.5 1.5 multiply_reduce_fusion
  9.0 14.4 %all_gather.36 = bf16[1024,256]{1,0:T(8,128)(2,1)} all-gather(bf16[256,256]{1,0:T(8,128)(2,1)S(1)} %get-tuple-element.8), channel_id=1, replica_groups=mesh['samp_0'=4,'samp_1'=2,'var_0'=8,'var_1'=4] {'var_1'}, dimensions={0}, use_global_device_ids=true | all-gather | bytes 655360 | tf_op jit(solution)/shard_map/all_gather | solution.py:22
  23.4 0.0 all-gather.11.cloned.1.call-update
  23.4 2.3 %gather_fusion.1 = bf16[256]{0:T(256)(128)(2,1)S(1)} fusion(f32[256,256]{1,0:T(8,128)S(1)} %bitcast.24, s32[256]{0:T(256)S(1)} %bitcast.25), kind=kCustom, calls=%fused_computation.1 | custom fusion | bytes 3072 | tf_op jit(solution)/shard_map/jit(diagonal)/cond/branch_0_fun/gather | solution.py:64
  25.8 8.5 %all-gather.4 = bf16[4,1,256]{2,1,0:T(2,128)(2,1)S(1)} all-gather(bf16[1,1,256]{2,1,0:T(2,128)(2,1)S(1)} %reshape.54), channel_id=1, replica_groups=mesh['samp_0'=4,'samp_1'=2,'var_0'=8,'var_1'=4] {'var_1'}, dimensions={0}, use_global_device_ids=true | all-gather | bytes 2560 | tf_op jit(solution)/shard_map/all_gather | solution.py:22
  34.4 24.0 %all_gather.39 = bf16[8192]{0:T(1024)(128)(2,1)S(1)} all-gather(bf16[1024]{0:T(1024)(128)(2,1)S(1)} %bitcast.28), channel_id=1, replica_groups=mesh['samp_0'=4,'samp_1'=2,'var_0'=8,'var_1'=4] {'var_0'}, dimensions={0}, use_global_device_ids=true | all-gather | bytes 18432 | tf_op jit(solution)/shard_map/all_gather | solution.py:22
  58.4 0.7 fusion.12
  59.1 0.0 copy-start.1
  59.1 38.2 %gather_fusion.2 = bf16[6144]{0:T(1024)(128)(2,1)S(1)} fusion(bf16[8192]{0:T(1024)(128)(2,1)S(1)} %all_gather.39, s32[6144]{0:T(1024)S(1)} %fusion.12), kind=kCustom, calls=%fused_computation.2 | custom fusion | bytes 49152 | tf_op jit(solution)/shard_map/jit(_take)/gather | solution.py:70
  97.3 0.0 copy-done.1
  97.4 12.3 %fusion = f32[1,1024]{1,0:T(1,128)S(1)} fusion(bf16[6144,1]{0,1:T(2,128)(2,1)S(1)} %reshape.68, bf16[6144,1024]{1,0:T(8,128)(2,1)} %param.9), kind=kOutput, calls=%fused_computation.3 | convolution fusion | flops 88080384 | bytes 12599296 | tf_op jit(solution)/shard_map/dot_general | solution.py:71
  109.7 0.6 broadcast_in_dim.35
  110.3 4.3 %all-to-all-start.1 = ((f32[8,1,1024]{2,1,0:T(1,128)}), f32[8,1,1024]{2,1,0:T(1,128)S(1)}, u32[]{:S(2)}, u32[]{:S(2)}) async-start(f32[8,1,1024]{2,1,0:T(1,128)} %broadcast_in_dim.35), calls=%async_computation.1 | async-start | bytes 65536 | tf_op jit(solution)/shard_map/all_to_all | solution.py:39
  114.6 0.0 all-gather.11.cloned.1.call-done
  114.6 22.1 %gather_fusion = bf16[6144,256]{1,0:T(8,128)(2,1)S(1)} fusion(bf16[8192,256]{1,0:T(8,128)(2,1)} %all-gather.11.cloned.1.call-done, s32[6144]{0:T(1024)S(1)} %fusion.12), kind=kCustom, calls=%fused_computation | custom fusion | bytes 6316032 | tf_op jit(solution)/shard_map/jit(_take)/gather | solution.py:66
  136.7 9.7 %fusion.7 = bf16[256,1024]{1,0:T(8,128)(2,1)} fusion(bf16[6144,1024]{1,0:T(8,128)(2,1)} %param.9, bf16[6144,256]{1,0:T(8,128)(2,1)S(1)} %gather_fusion, pred[6144]{0:T(1024)(128)(4,1)S(1)} %get-tuple-element.6), kind=kOutput, calls=%fused_computation.10 | convolution fusion | flops 3223060480 | bytes 16259072 | tf_op jit(solution)/shard_map/dot_general | solution.py:67
  146.4 0.0 all-to-all-done.1
  146.4 4.8 %all-to-all-start = ((bf16[8,1024,32]{1,2,0:T(8,128)(2,1)}), bf16[8,1024,32]{1,2,0:T(8,128)(2,1)S(1)}, u32[]{:S(2)}, u32[]{:S(2)}) async-start(bf16[8,1024,32]{1,2,0:T(8,128)(2,1)} %bitcast.26), calls=%async_computation | async-start | bytes 1048576 | tf_op jit(solution)/shard_map/all_to_all | solution.py:33
  151.2 12.5 %all-gather.5 = f32[4,1,256]{2,1,0:T(1,128)S(1)} all-gather(f32[1,1,256]{2,1,0:T(1,128)S(1)} %bitcast.30), channel_id=2, replica_groups=mesh['samp_0'=4,'samp_1'=2,'var_0'=8,'var_1'=4] {'samp_0'}, dimensions={0}, use_global_device_ids=true | all-gather | bytes 5120 | tf_op jit(solution)/shard_map/all_gather | solution.py:15
  163.7 1.8 all-gather.6
  165.5 14.5 %all-gather.7 = f32[8,1,256]{2,1,0:T(1,128)S(1)} all-gather(f32[1,1,256]{2,1,0:T(1,128)S(1)} %bitcast.31), channel_id=4, replica_groups=mesh['samp_0'=4,'samp_1'=2,'var_0'=8,'var_1'=4] {'var_0'}, dimensions={0}, use_global_device_ids=true | all-gather | bytes 9216 | tf_op jit(solution)/shard_map/all_gather | solution.py:15
  180.0 10.1 %all-gather.8 = f32[4,1,256]{2,1,0:T(1,128)S(1)} all-gather(f32[1,1,256]{2,1,0:T(1,128)S(1)} %bitcast.32), channel_id=5, replica_groups=mesh['samp_0'=4,'samp_1'=2,'var_0'=8,'var_1'=4] {'var_1'}, dimensions={0}, use_global_device_ids=true | all-gather | bytes 5120 | tf_op jit(solution)/shard_map/all_gather | solution.py:15
  190.1 0.1 dynamic_slice.3
  190.2 0.0 all-to-all-done
  190.2 0.1 convert_reduce_fusion
  190.3 0.8 rsqrt_multiply_fusion
  (12 shorter events, 0.2 us)
Async XLA Ops:
  6.5 1.0 copy-start
  6.5 108.1 %all-gather.11.cloned.1.call-start = ((), (), s32[]{:S(2)}) async-start(), calls=%async_computation.2 | async-start | bytes 4718592 | tf_op jit(solution)/shard_map/all_gather | solution.py:22
  59.1 38.2 %copy-start.1 = (s32[6144]{0:T(1024)S(1)}, s32[6144]{0:T(1024)}, u32[]{:S(2)}) copy-start(s32[6144]{0:T(1024)} %param.8) | copy-start | bytes 73732
  110.3 36.1 %all-to-all-start.1 = ((f32[8,1,1024]{2,1,0:T(1,128)}), f32[8,1,1024]{2,1,0:T(1,128)S(1)}, u32[]{:S(2)}, u32[]{:S(2)}) async-start(f32[8,1,1024]{2,1,0:T(1,128)} %broadcast_in_dim.35), calls=%async_computation.1 | async-start | bytes 65536 | tf_op jit(solution)/shard_map/all_to_all | solution.py:39
  146.4 43.8 %all-to-all-start = ((bf16[8,1024,32]{1,2,0:T(8,128)(2,1)}), bf16[8,1024,32]{1,2,0:T(8,128)(2,1)S(1)}, u32[]{:S(2)}, u32[]{:S(2)}) async-start(bf16[8,1024,32]{1,2,0:T(8,128)(2,1)} %bitcast.26), calls=%async_computation | async-start | bytes 1048576 | tf_op jit(solution)/shard_map/all_to_all | solution.py:33
Sparse Core Ops, SparseCore 0:
  23.5 57.5 all-gather.10
